TPU v7x, 512 devices: a whole 4x4x16 slice. The times are simulated.
512 devices in a mesh: seq: 32 (over z, core), mp: 16 (over y, x).
Axes of the slice: x: 4, y: 4, z: 16, core: 2. Of those that a mesh axis runs over, the one named last changes fastest.
Arguments:
- continued_prompt_entries: bfloat16 [4096, 4096], P('seq', 'mp'), may hold values from -6 to 6
- padded_prompt_entries: bfloat16 [4096, 4096], P('seq', 'mp'), may hold values from -6 to 6
- prompt_live_extents: int32 [64], P('seq'), may hold values from 8 to 64, as said below
- preceding_entry_line: bfloat16 [4096], P('mp'), may hold values from -6 to 6
- carried_memory: float32 [64, 64, 64], P('mp'), may hold values from -24 to 24
- token_mixing_ratios: float32 [5, 4096], replicated, may hold values from 0.05 to 0.95
- acceptance_transform: bfloat16 [4096, 4096], P('seq', 'mp'), may hold values from -0.09375 to 0.09375
- lookup_transform: bfloat16 [4096, 4096], P('seq', 'mp'), may hold values from -0.09375 to 0.09375
- payload_transform: bfloat16 [4096, 4096], P('seq', 'mp'), may hold values from -0.09375 to 0.09375
- gating_transform: bfloat16 [4096, 4096], P('seq', 'mp'), may hold values from -0.09375 to 0.09375
- fading_baseline: float32 [4096], P('mp'), may hold values from -10 to -3.5
- fading_left_factor: bfloat16 [4096, 128], replicated, may hold values from -0.09375 to 0.09375
- fading_right_factor: bfloat16 [128, 4096], P(None, 'mp'), may hold values from -0.5 to 0.5
- present_reward: float32 [64, 64], P('mp'), may hold values from -3 to 3
- group_layer_scaling: float32 [4096], P('mp'), may hold values from 0.5 to 1.5
- group_layer_shift_term: float32 [4096], P('mp'), may hold values from -1.8 to 1.8
- final_transform: bfloat16 [4096, 4096], P('mp', 'seq'), may hold values from -0.09375 to 0.09375
Outputs:
- mixed: bfloat16 [32, 256, 4096], P('seq', 'mp')
- span_states: float32 [32, 64, 64, 64], P('seq', 'mp')
- request_states: float32 [64, 64, 64, 64], P('seq', 'mp')
Inputs may be any that keep to these rules, and one draw needn't show every extreme that they name: `prompt_live_extents`: some request has all 64 rows live.
All inputs are finite; a program needn't handle non-finite values.
Results may differ from a plain program's by a relative error of at most 0.0076.
Values may be sent and summed in bfloat16 or wider, within the bound.
A program may use at most 64 MiB of HBM per device.

v0:
```python
import jax
import jax.numpy as jnp
from jax import lax
from jax.sharding import PartitionSpec as P

BLK = 64
norm_eps = 0.00064
highest = lax.Precision.HIGHEST


def passed_along(x, axis, by):
    length = lax.axis_size(axis)
    pairs = [(i, i + by) for i in range(length) if 0 <= i + by < length]
    return lax.ppermute(x, axis, pairs)


def entering(value, axis, join, neutral):
    count, mine = (lax.axis_size(axis), lax.axis_index(axis))
    pieces = jax.tree.map(lambda part: lax.all_gather(part, axis), value)
    total = jax.tree.map(
        lambda part, zero: jnp.full_like(part, 0) + jnp.asarray(zero, part.dtype), value, neutral
    )

    def hop(position, total):
        longer = join(total, jax.tree.map(lambda part: part[position], pieces))
        return jax.tree.map(lambda new, old: jnp.where(position < mine, new, old), longer, total)

    return lax.fori_loop(0, count - 1, hop, total)


def mix_rows(current, previous, weight):
    here = current.astype(jnp.float32)
    return (here + weight[None, :] * (previous.astype(jnp.float32) - here)).astype(jnp.bfloat16)


def block_sweep(
    evolving_memory,
    acceptance_entries,
    lookup_entries,
    payload_entries,
    log_fading_amount,
    diagonal_reward,
):
    inclusive = jnp.cumsum(log_fading_amount, axis=0)
    exclusive = inclusive - log_fading_amount
    recept_scaled = acceptance_entries * jnp.exp(exclusive)
    keys_scaled = lookup_entries * jnp.exp(-inclusive)
    scores = jnp.einsum("ihc,jhc->hij", recept_scaled, keys_scaled, precision=highest)
    count = acceptance_entries.shape[0]
    row_index = lax.broadcasted_iota(jnp.int32, (count, count), 0)
    col_index = lax.broadcasted_iota(jnp.int32, (count, count), 1)
    scores = jnp.where((row_index > col_index)[None], scores, 0.0)
    diagonal_contribution = jnp.sum(
        acceptance_entries * diagonal_reward[None] * lookup_entries, axis=-1, keepdims=True
    )
    answer_lines = (
        jnp.einsum("hij,jhd->ihd", scores, payload_entries, precision=highest)
        + diagonal_contribution * payload_entries
    )
    answer_lines = answer_lines + jnp.einsum(
        "ihc,hcd->ihd", recept_scaled, evolving_memory, precision=highest
    )
    total = inclusive[-1]
    carried = lookup_entries * jnp.exp(total[None] - inclusive)
    new_state = jnp.exp(total)[:, :, None] * evolving_memory + jnp.einsum(
        "jhc,jhd->hcd", carried, payload_entries, precision=highest
    )
    return (new_state, answer_lines)


def continued_recurrence(
    acceptance_entries, lookup_entries, payload_entries, log_fading_amount, diagonal_reward
):
    length, per_group_view, embedding_dimension = acceptance_entries.shape
    blocks = length // BLK

    def step(evolving_memory, entry_lines):
        return block_sweep(
            evolving_memory,
            entry_lines[0],
            entry_lines[1],
            entry_lines[2],
            entry_lines[3],
            diagonal_reward,
        )

    shaped = tuple(
        (
            a.reshape(blocks, BLK, per_group_view, embedding_dimension)
            for a in (acceptance_entries, lookup_entries, payload_entries, log_fading_amount)
        )
    )
    evolving_memory, results = lax.scan(
        step,
        jnp.zeros((per_group_view, embedding_dimension, embedding_dimension), jnp.float32),
        shaped,
    )
    return (evolving_memory, results.reshape(length, per_group_view, embedding_dimension))


def combine(earlier, later):
    return (earlier[0] + later[0], jnp.exp(later[0])[:, :, None] * earlier[1] + later[1])


def shifted_rows(current, edge_row, long_rows, requests, slot_rows):
    feature_part = current.shape[1]
    long_prev = jnp.concatenate([edge_row, current[: long_rows - 1]], axis=0)
    short_view = current[long_rows:].reshape(requests, slot_rows, feature_part)
    short_prev = jnp.concatenate(
        [jnp.zeros((requests, 1, feature_part), current.dtype), short_view[:, :-1]], axis=1
    )
    short_prev = short_prev.reshape(requests * slot_rows, feature_part)
    return jnp.concatenate([long_prev, short_prev], axis=0)


def on_device(
    continued_prompt_entries,
    padded_prompt_entries,
    prompt_live_extents,
    preceding_entry_line,
    carried_memory,
    token_mixing_ratios,
    acceptance_transform,
    lookup_transform,
    payload_transform,
    gating_transform,
    fading_baseline,
    fading_left_factor,
    fading_right_factor,
    present_reward,
    group_layer_scaling,
    group_layer_shift_term,
    final_transform,
):
    long_rows = continued_prompt_entries.shape[0]
    requests = prompt_live_extents.shape[0]
    slot_rows = padded_prompt_entries.shape[0] // requests
    per_group_view, embedding_dimension = present_reward.shape
    arrived = passed_along(continued_prompt_entries[-1:], "seq", 1)
    first = lax.axis_index("seq") == 0
    edge_row = jnp.where(first, preceding_entry_line[None, :], arrived)
    current = jnp.concatenate([continued_prompt_entries, padded_prompt_entries], axis=0)
    current, edge_full = (
        lax.all_gather(current, "mp", axis=1, tiled=True),
        lax.all_gather(edge_row, "mp", axis=1, tiled=True),
    )
    previous = shifted_rows(current, edge_full, long_rows, requests, slot_rows)
    mixes = [mix_rows(current, previous, token_mixing_ratios[index]) for index in range(5)]
    total_rows = current.shape[0]
    columns = acceptance_transform.shape[1]
    pieces = (
        lax.all_gather(acceptance_transform, "seq", axis=0, tiled=True),
        lax.all_gather(lookup_transform, "seq", axis=0, tiled=True),
        lax.all_gather(payload_transform, "seq", axis=0, tiled=True),
        lax.all_gather(gating_transform, "seq", axis=0, tiled=True),
    )
    acceptance_entries, lookup_entries, payload_entries, gate = tuple(
        (
            jnp.dot(source, piece, preferred_element_type=jnp.float32)
            for source, piece in zip(mixes[:4], pieces)
        )
    )
    squeezed = jnp.tanh(
        jnp.dot(mixes[4], fading_left_factor, preferred_element_type=jnp.float32)
    ).astype(jnp.bfloat16)
    log_fading_amount = -jnp.exp(
        fading_baseline[None, :]
        + jnp.dot(squeezed, fading_right_factor, preferred_element_type=jnp.float32)
    )
    recept3, keys3, values3, decay3 = [
        a.reshape(total_rows, per_group_view, embedding_dimension)
        for a in (acceptance_entries, lookup_entries, payload_entries, log_fading_amount)
    ]
    local_state, long_out = continued_recurrence(
        recept3[:long_rows],
        keys3[:long_rows],
        values3[:long_rows],
        decay3[:long_rows],
        present_reward,
    )
    long_decay = decay3[:long_rows]
    group_total = jnp.sum(long_decay, axis=0)
    blank = (
        jnp.zeros((per_group_view, embedding_dimension), jnp.float32),
        jnp.zeros((per_group_view, embedding_dimension, embedding_dimension), jnp.float32),
    )
    prefix_total, prefix_state = entering((group_total, local_state), "seq", combine, blank)
    incoming = jnp.exp(prefix_total)[:, :, None] * carried_memory + prefix_state
    before_row = jnp.cumsum(long_decay, axis=0) - long_decay
    long_out = long_out + jnp.einsum(
        "ihc,hcd->ihd", recept3[:long_rows] * jnp.exp(before_row), incoming, precision=highest
    )
    span_end = jnp.exp(group_total)[:, :, None] * incoming + local_state
    live_rows = (
        lax.broadcasted_iota(jnp.int32, (requests, slot_rows), 1) < prompt_live_extents[:, None]
    )
    live_flat = live_rows.reshape(requests * slot_rows).astype(jnp.float32)[:, None, None]
    short_shape = (requests, slot_rows, per_group_view, embedding_dimension)
    short_recept = recept3[long_rows:].reshape(short_shape)
    short_keys = (keys3[long_rows:] * live_flat).reshape(short_shape)
    short_values = values3[long_rows:].reshape(short_shape)
    short_decay = (decay3[long_rows:] * live_flat).reshape(short_shape)
    zeroed_memory = jnp.zeros(
        (per_group_view, embedding_dimension, embedding_dimension), jnp.float32
    )

    def request_pass(acceptance_lines, lookup_table, payload_table, fading_table):
        return block_sweep(
            zeroed_memory,
            acceptance_lines,
            lookup_table,
            payload_table,
            fading_table,
            present_reward,
        )

    request_states, short_out = jax.vmap(request_pass)(
        short_recept, short_keys, short_values, short_decay
    )
    wkv = jnp.concatenate(
        [long_out, short_out.reshape(requests * slot_rows, per_group_view, embedding_dimension)],
        axis=0,
    )
    mean = jnp.mean(wkv, axis=-1, keepdims=True)
    centred = wkv - mean
    variance = jnp.mean(centred * centred, axis=-1, keepdims=True)
    normed = (centred * lax.rsqrt(variance + norm_eps)).reshape(
        total_rows, columns
    ) * group_layer_scaling[None, :] + group_layer_shift_term[None, :]
    row_live = jnp.concatenate(
        [jnp.ones((long_rows,), dtype=bool), live_rows.reshape(requests * slot_rows)], axis=0
    )
    hidden = jnp.where(row_live[:, None], normed * jax.nn.silu(gate), 0.0).astype(jnp.bfloat16)
    full_out = lax.all_gather(final_transform, "seq", axis=1, tiled=True)
    mixed_rows = lax.psum_scatter(
        jnp.dot(hidden, full_out, preferred_element_type=jnp.float32),
        "mp",
        scatter_dimension=0,
        tiled=True,
    )
    return (mixed_rows.astype(jnp.bfloat16)[None], span_end[None], request_states)


def solution(mesh):
    placed = (
        P("seq", "mp"),
        P("seq", "mp"),
        P("seq"),
        P("mp"),
        P("mp", None, None),
        P(),
        P("seq", "mp"),
        P("seq", "mp"),
        P("seq", "mp"),
        P("seq", "mp"),
        P("mp"),
        P(),
        P(None, "mp"),
        P("mp", None),
        P("mp"),
        P("mp"),
        P("mp", "seq"),
    )
    return jax.shard_map(
        on_device,
        mesh=mesh,
        in_specs=placed,
        out_specs=(P("seq", "mp", None), P("seq", "mp", None, None), P("seq", "mp", None, None)),
        check_vma=False,
    )
```

profile of v0, /device:TPU:2, one launch (start us, length us, event | category | flops | bytes accessed | tf_op | source)
XLA Modules:
  0.0 631.1 jit_solution(9215683122175775181)
XLA Ops:
  7.2 1.6 pad_maximum_fusion.2
  11.7 1.7 collective-permute-start
  13.4 1.9 fusion.85
  16.0 27.3 %all_gather.34 = bf16[1,4096]{1,0:T(2,128)(2,1)} all-gather(bf16[1,256]{1,0:T(2,128)(2,1)S(1)} %broadcast_select_fusion), channel_id=1, replica_groups=mesh['seq'=32,'mp'=16] {'mp'}, dimensions={1}, use_global_device_ids=true | all-gather | bytes 8704 | tf_op jit(solution)/shard_map/all_gather | solution.py:145
  43.3 35.5 %all-gather.9.cloned.1.call-done = bf16[256,4096]{1,0:T(8,128)(2,1)} async-done(((bf16[256,256]{1,0:T(8,128)(2,1)}), bf16[256,4096]{1,0:T(8,128)(2,1)}) %all-gather.9.cloned.1.call-update) | async-done | bytes 2097168 | tf_op jit(solution)/shard_map/all_gather | solution.py:144
  78.7 1.5 slice.100
  80.2 1.2 concatenate.24
  82.5 3.0 fusion.41
  85.5 1.3 slice_reduce_fusion
  87.9 64.6 %all-gather.15.cloned.1.call-done = bf16[4096,256]{1,0:T(8,128)(2,1)} async-done(((bf16[128,256]{1,0:T(8,128)(2,1)}), bf16[4096,256]{1,0:T(8,128)(2,1)}) %all-gather.15.cloned.1.call-update) | async-done | bytes 2097168 | tf_op jit(solution)/shard_map/all_gather | solution.py:152
  152.5 3.7 fusion.25
  157.0 66.3 %all-gather.11.cloned.1.call-done = bf16[4096,256]{1,0:T(8,128)(2,1)} async-done(((bf16[128,256]{1,0:T(8,128)(2,1)}), bf16[4096,256]{1,0:T(8,128)(2,1)}) %all-gather.11.cloned.1.call-update) | async-done | bytes 2097168 | tf_op jit(solution)/shard_map/all_gather | solution.py:153
  223.3 4.0 fusion.29
  228.2 65.8 %all-gather.13.cloned.1.call-done = bf16[4096,256]{1,0:T(8,128)(2,1)} async-done(((bf16[128,256]{1,0:T(8,128)(2,1)}), bf16[4096,256]{1,0:T(8,128)(2,1)}) %all-gather.13.cloned.1.call-update) | async-done | bytes 2097168 | tf_op jit(solution)/shard_map/all_gather | solution.py:154
  294.0 3.6 fusion.27
  298.5 13.3 %while.29 = (s32[]{:T(128)}, f32[4,64,64]{2,1,0:T(8,128)S(1)}, f32[2,64,4,64]{1,0,3,2:T(2,128)}, f32[2,64,4,64]{1,0,3,2:T(2,128)S(1)}, f32[2,64,4,64]{3,2,1,0:T(...) while((s32[]{:T(128)}, f32[4,64,64]{2,1,0:T(8,128)S(1)}, ...), condition=%wide.region_3.4_spmd.clone, body=%wide.region_0.3_spmd.clone.sunk | while | flops 51646208 | bytes 2444416 | solution.py:93
  300.4 4.3 dynamic_update_slice.6
  307.1 4.3 dynamic_update_slice.6
  314.7 32.2 %all_gather.39 = f32[32,4,64]{2,1,0:T(4,128)} all-gather(f32[1,4,64]{2,1,0:T(4,128)S(1)} %all_gather.38), channel_id=1, replica_groups=mesh['seq'=32,'mp'=16] {'seq'}, dimensions={0}, use_global_device_ids=true | all-gather | bytes 33792 | tf_op jit(solution)/shard_map/all_gather | solution.py:19
  347.6 1.2 reshape.144
  358.3 25.6 %all-gather.21.cloned.1.call-done = f32[128,64,64]{2,1,0:T(8,128)} async-done(((f32[4,64,64]{2,1,0:T(8,128)}), f32[128,64,64]{2,1,0:T(8,128)}) %all-gather.21.cloned.1.call-update) | async-done | bytes 2097168 | tf_op jit(solution)/shard_map/all_gather | solution.py:19
  383.9 53.9 %while.30 = (s32[]{:T(128)}, f32[4,64]{1,0:T(4,128)S(1)}, f32[4,64,64]{2,1,0:T(8,128)S(1)}, s32[]{:T(128)}, f32[32,4,64]{2,1,0:T(4,128)}, /*index=5*/f32[32,4,64,64]{3,2,1,0:T(8,128)}, s32[]{:T(128)}, s32[]{:T(128)}) while((s32[]{:T(128)}, f32[4,64]{1,0:T(4,128)S(1)}, f32[4,64,64]{2,1,0:T(8,128)S(1)}, s32[]{:T(128)}, ...), condition=%wide.region_6.7_spmd.clone, body=%wide.region_5.6_spmd.clone.sunk | while | flops 66308 | bytes 201843 | solution.py:28
  437.8 1.8 fusion.42
  442.3 1.8 copy.102
  444.8 1.8 copy.101
  446.5 1.7 copy.99
  448.2 5.8 all-gather.17.cloned.1.call-done
  454.0 72.6 %all-gather.19.cloned.1.call-done = bf16[256,4096]{1,0:T(8,128)(2,1)} async-done(((bf16[256,128]{1,0:T(8,128)(2,1)}), bf16[256,4096]{1,0:T(8,128)(2,1)}) %all-gather.19.cloned.1.call-update) | async-done | bytes 2097168 | tf_op jit(solution)/shard_map/all_gather | solution.py:234
  526.5 7.5 %fusion.63 = f32[256,4096]{1,0:T(8,128)} fusion(bf16[256,4096]{1,0:T(8,128)(2,1)} %all-gather.19.cloned.1.call-done, f32[256,256]{1,0:T(8,128)} %copy.102, f32[256,256]{1,0:T(8,128)} %copy.101, f32[128,256]{1,0:T(8,128)} %concatenate.27, f32[128,256]{1,0:T(8,128)} %copy.99, bf16[4096,256]{1,0:T(8,128)(2,1)} %all-gather.17.cloned.1.call-done, ...), kind=kOutput, calls=%fused_computation.83 | convolution fusion | flops 1086062592 | bytes 13388032 | tf_op jit(solution)/shard_map/dot_general | solution.py:236
  535.0 1.3 convolution_add_fusion.1
  537.1 85.6 %reduce-scatter.2.cloned.1.call-done = f32[16,4096]{1,0:T(8,128)} async-done(((f32[256,4096]{1,0:T(8,128)}), f32[16,4096]{1,0:T(8,128)}) %reduce-scatter.2.cloned.1.call-update) | async-done | bytes 262160 | tf_op jit(solution)/shard_map/reduce_scatter | solution.py:235
  622.7 1.6 convert_bitcast_fusion
  (196 shorter events, 83.7 us)
Async XLA Ops:
  7.2 75.3 %copy-start = (bf16[4096,128]{1,0:T(8,128)(2,1)S(1)}, bf16[4096,128]{1,0:T(8,128)(2,1)}, u32[]{:S(2)}) copy-start(bf16[4096,128]{1,0:T(8,128)(2,1)} %param.32) | copy-start | bytes 3145732
  7.2 71.5 %all-gather.9.cloned.1.call-start = ((), (), s32[]{:S(2)}) async-start(), calls=%async_computation.1 | async-start | bytes 2228224 | tf_op jit(solution)/shard_map/all_gather | solution.py:144
  8.9 143.6 %all-gather.15.cloned.1.call-start = ((), (), s32[]{:S(2)}) async-start(), calls=%async_computation.4 | async-start | bytes 2162688 | tf_op jit(solution)/shard_map/all_gather | solution.py:152
  9.6 213.7 %all-gather.11.cloned.1.call-start = ((), (), s32[]{:S(2)}) async-start(), calls=%async_computation.2 | async-start | bytes 2162688 | tf_op jit(solution)/shard_map/all_gather | solution.py:153
  10.4 283.7 %all-gather.13.cloned.1.call-start = ((), (), s32[]{:S(2)}) async-start(), calls=%async_computation.3 | async-start | bytes 2162688 | tf_op jit(solution)/shard_map/all_gather | solution.py:154
  10.9 372.9 %all-gather.21.cloned.1.call-start = ((), (), s32[]{:S(2)}) async-start(), calls=%async_computation.8 | async-start | bytes 4325376 | tf_op jit(solution)/shard_map/all_gather | solution.py:19
  11.7 3.7 collective-permute-start
  78.7 2.7 copy-start.3
  223.3 70.7 %copy-start.8 = (bf16[2,64,4096]{2,1,0:T(8,128)(2,1)S(1)}, bf16[2,64,4096]{2,1,0:T(8,128)(2,1)}, u32[]{:S(2)}) copy-start(bf16[2,64,4096]{2,1,0:T(8,128)(2,1)} %concatenate.24) | copy-start | bytes 3145732
  223.3 70.7 %copy-start.14 = (bf16[1,4096]{1,0:T(2,128)(2,1)S(1)}, bf16[1,4096]{1,0:T(2,128)(2,1)}, u32[]{:S(2)}) copy-start(bf16[1,4096]{1,0:T(2,128)(2,1)} %all_gather.34) | copy-start | bytes 24580
  294.0 4.5 copy-start.13
  298.5 15.4 %copy-start.16 = (s32[2]{0:T(128)S(1)}, s32[2]{0:T(128)}, u32[]{:S(2)}) copy-start(s32[2]{0:T(128)} %param.23) | copy-start | bytes 28
  298.5 16.1 %copy-start.15 = (f32[256]{0:T(256)S(1)}, f32[256]{0:T(256)}, u32[]{:S(2)}) copy-start(f32[256]{0:T(256)} %get-tuple-element.272) | copy-start | bytes 3076
  298.5 48.3 %copy-start.6 = (f32[128,256]{0,1:T(8,128)S(1)}, f32[128,256]{0,1:T(8,128)}, u32[]{:S(2)}) copy-start(f32[128,256]{0,1:T(8,128)} %get-tuple-element.274) | copy-start | bytes 393220
  298.5 48.5 %copy-start.10 = (f32[128,256]{0,1:T(8,128)S(1)}, f32[128,256]{0,1:T(8,128)}, u32[]{:S(2)}) copy-start(f32[128,256]{0,1:T(8,128)} %get-tuple-element.273) | copy-start | bytes 393220
  311.8 0.7 copy-start.1
  312.5 141.5 %all-gather.17.cloned.1.call-start = ((), (), s32[]{:S(2)}) async-start(), calls=%async_computation.5 | async-start | bytes 2162688 | tf_op jit(solution)/shard_map/all_gather | solution.py:155
  313.0 213.5 %all-gather.19.cloned.1.call-start = ((), (), s32[]{:S(2)}) async-start(), calls=%async_computation.6 | async-start | bytes 2162688 | tf_op jit(solution)/shard_map/all_gather | solution.py:234
  313.8 308.9 %reduce-scatter.2.cloned.1.call-start = ((), (), s32[]{:S(2)}) async-start(), calls=%async_computation.7 | async-start | bytes 4456448 | tf_op jit(solution)/shard_map/reduce_scatter | solution.py:235
  347.3 7.4 %copy-start.12 = (f32[2,64,4,64]{1,0,3,2:T(2,128)S(1)}, f32[2,64,4,64]{1,0,3,2:T(2,128)}, u32[]{:S(2)}) copy-start(f32[2,64,4,64]{1,0,3,2:T(2,128)} %get-tuple-element.156) | copy-start | bytes 393220
  347.5 5.4 copy-start.7
  354.6 171.9 %copy-start.17 = (f32[256]{0:T(256)S(1)}, f32[256]{0:T(256)}, u32[]{:S(2)}) copy-start(f32[256]{0:T(256)} %param.36) | copy-start | bytes 3076
  358.3 168.2 %copy-start.4 = (bf16[256,4096]{1,0:T(8,128)(2,1)S(1)}, bf16[256,4096]{1,0:T(8,128)(2,1)}, u32[]{:S(2)}) copy-start(bf16[256,4096]{1,0:T(8,128)(2,1)} %all-gather.9.cloned.1.call-done) | copy-start | bytes 6291460
  439.6 1.0 copy-start.5
  534.0 0.9 copy-start.9
  534.0 2.3 copy-start.2
  534.0 2.3 copy-start.11
Sparse Core Ops, SparseCore 0:
  11.6 67.0 all-gather.8
  80.8 71.5 all-gather.14
  154.6 68.6 all-gather.10
  225.3 68.6 all-gather.12
  312.6 71.2 all-gather.20
  385.8 68.0 all-gather.16
  456.0 70.4 all-gather.18
  534.2 88.4 reduce-scatter.1
where the time goes:
time: 633 us; the launch traced here: 631 us
  waiting for transfers between devices  425 us (67%)
  other arithmetic  64.5 us (10%)
  blocking collectives  59.4 us (9%)
  local copies, waits for them, and re-layouts  35.3 us (6%)
  matrix products  29.4 us (5%)
  between operations  14.5 us (2%)
    reduce_scatter x1, waiting for transfers between devices, on_device(): lax.psum_scatter(jnp.dot(hidden, full_out, preferred_element_type=jnp.flo...  85.6 us
    all_gather x1, waiting for transfers between devices, on_device(): full_out = lax.all_gather(final_transform, 'seq', axis=1, tiled=True)  72.6 us
    all_gather x1, waiting for transfers between devices, on_device(): lax.all_gather(lookup_transform, 'seq', axis=0, tiled=True)  66.3 us
    all_gather x1, waiting for transfers between devices, on_device(): lax.all_gather(payload_transform, 'seq', axis=0, tiled=True)  65.8 us
    all_gather x1, waiting for transfers between devices, on_device(): lax.all_gather(acceptance_transform, 'seq', axis=0, tiled=True)  64.6 us
    all_gather x1, waiting for transfers between devices, on_device(): lax.all_gather(current, 'mp', axis=1, tiled=True)  35.5 us
    all_gather x1, blocking collectives, entering(): pieces = jax.tree.map(lambda part: lax.all_gather(part, axis), value)  32.2 us
    select_n x31, other arithmetic, hop(): jnp.where(position < mine, new, old)  32 us
  transfers between devices with their start and end apart: 9, of which 8 were waited for; matrix products, arithmetic and copies ran while one was open for 16% of the time, Pallas kernels for 0%

commit v1 on v0

--- a/solution.py
+++ b/solution.py
@@ -6,6 +6,11 @@
 BLK = 64
 norm_eps = 0.00064
 highest = lax.Precision.HIGHEST
+
+
+def tiled_gather(array, axis, dim):
+    copies = jnp.concatenate([array] * lax.axis_size(axis), axis=dim)
+    return lax.all_to_all(copies, axis, dim, dim, tiled=True)
 
 
 def passed_along(x, axis, by):
@@ -141,7 +146,7 @@
     edge_row = jnp.where(first, preceding_entry_line[None, :], arrived)
     current = jnp.concatenate([continued_prompt_entries, padded_prompt_entries], axis=0)
     current, edge_full = (
-        lax.all_gather(current, "mp", axis=1, tiled=True),
+        tiled_gather(current, "mp", 1),
         lax.all_gather(edge_row, "mp", axis=1, tiled=True),
     )
     previous = shifted_rows(current, edge_full, long_rows, requests, slot_rows)

time: 633 us -> 573 us (0.905)
  waiting for transfers between devices: 425 us -> 324 us
  local copies, waits for them, and re-layouts: 35.3 us -> 48.9 us
  blocking collectives: 59.4 us -> 71.9 us
  starting transfers between devices: 2.04 us -> 11.1 us
  matrix products: 29.4 us -> 35.8 us
    all_gather x1, waiting for transfers between devices: 64.6 us -> 0.02 us  [on_device(): lax.all_gather(acceptance_transform, 'seq', axis=0, tiled=True)]
    all_gather x1 -> x0, waiting for transfers between devices: 35.5 us -> none  [on_device(): lax.all_gather(current, 'mp', axis=1, tiled=True)]
    all_gather x1, blocking collectives: 27.3 us -> 40.2 us  [on_device(): lax.all_gather(edge_row, 'mp', axis=1, tiled=True)]
    all_to_all x0 -> x1, starting transfers between devices: none -> 9.55 us  [tiled_gather(): return lax.all_to_all(copies, axis, dim, dim, tiled=True)]
  transfers between devices with their start and end apart: 9 -> 9, of which waited for: 8 -> 7; matrix products, arithmetic and copies ran while one was open for 16% -> 20% of each run, Pallas kernels for 0% -> 0%
where the time goes in v1:
time: 573 us; the launch traced here: 570 us
  waiting for transfers between devices  324 us (57%)
  blocking collectives  71.9 us (13%)
  other arithmetic  62.9 us (11%)
  local copies, waits for them, and re-layouts  48.9 us (9%)
  matrix products  35.8 us (6%)
  between operations  14.7 us (3%)
  starting transfers between devices  11.1 us (2%)
    reduce_scatter x1, waiting for transfers between devices, on_device(): lax.psum_scatter(jnp.dot(hidden, full_out, preferred_element_type=jnp.flo...  85.1 us
    all_gather x1, waiting for transfers between devices, on_device(): full_out = lax.all_gather(final_transform, 'seq', axis=1, tiled=True)  72.5 us
    all_gather x1, waiting for transfers between devices, on_device(): lax.all_gather(payload_transform, 'seq', axis=0, tiled=True)  65.3 us
    all_gather x1, waiting for transfers between devices, on_device(): lax.all_gather(lookup_transform, 'seq', axis=0, tiled=True)  64.3 us
    all_gather x1, blocking collectives, on_device(): lax.all_gather(edge_row, 'mp', axis=1, tiled=True)  40.2 us
    select_n x31, other arithmetic, hop(): jnp.where(position < mine, new, old)  32 us
    all_gather x1, blocking collectives, entering(): pieces = jax.tree.map(lambda part: lax.all_gather(part, axis), value)  31.8 us
    all_gather x1, waiting for transfers between devices, entering(): pieces = jax.tree.map(lambda part: lax.all_gather(part, axis), value)  26.7 us
  transfers between devices with their start and end apart: 9, of which 7 were waited for; matrix products, arithmetic and copies ran while one was open for 20% of the time, Pallas kernels for 0%

profile of v1, /device:TPU:2, one launch (start us, length us, event | category | flops | bytes accessed | tf_op | source)
XLA Modules:
  0.0 570.2 jit_solution(7174210874886913070)
XLA Ops:
  11.0 2.4 copy.154
  13.4 9.5 %all-to-all-start = ((bf16[256,16,256]{2,0,1:T(8,128)(2,1)}), bf16[256,16,256]{2,0,1:T(8,128)(2,1)S(1)}, u32[]{:S(2)}, u32[]{:S(2)}) async-start(bf16[256,16,256]{2,0,1:T(8,128)(2,1)} %copy.154), calls=%async_computation | async-start | bytes 4194304 | tf_op jit(solution)/shard_map/all_to_all | solution.py:13
  26.9 40.2 %all_gather.30 = bf16[1,4096]{0,1:T(8,128)(2,1)} all-gather(bf16[1,256]{0,1:T(8,128)(2,1)S(1)} %reshape_select_fusion), channel_id=1, replica_groups=mesh['seq'=32,'mp'=16] {'mp'}, dimensions={1}, use_global_device_ids=true | all-gather | bytes 8704 | tf_op jit(solution)/shard_map/all_gather | solution.py:150
  67.1 1.6 copy.159
  68.7 2.3 reshape.143
  71.0 2.5 concatenate.28
  73.5 2.3 copy.160
  75.8 2.4 copy.155
  78.2 2.5 slice.104
  80.7 4.3 fusion.41
  87.4 5.0 fusion.25
  93.1 64.3 %all-gather.8.cloned.1.call-done = bf16[4096,256]{1,0:T(8,128)(2,1)} async-done(((bf16[128,256]{1,0:T(8,128)(2,1)}), bf16[4096,256]{1,0:T(8,128)(2,1)}) %all-gather.8.cloned.1.call-update) | async-done | bytes 2097168 | tf_op jit(solution)/shard_map/all_gather | solution.py:158
  157.4 4.8 fusion.29
  162.9 65.3 %all-gather.10.cloned.1.call-done = bf16[4096,256]{1,0:T(8,128)(2,1)} async-done(((bf16[128,256]{1,0:T(8,128)(2,1)}), bf16[4096,256]{1,0:T(8,128)(2,1)}) %all-gather.10.cloned.1.call-update) | async-done | bytes 2097168 | tf_op jit(solution)/shard_map/all_gather | solution.py:159
  228.3 4.8 fusion.27
  235.4 13.5 %while.29 = (s32[]{:T(128)}, f32[4,64,64]{2,1,0:T(8,128)S(1)}, f32[2,64,4,64]{1,0,3,2:T(2,128)}, f32[2,64,4,64]{1,0,3,2:T(2,128)S(1)}, f32[2,64,4,64]{3,2,1,0:T(...) while((s32[]{:T(128)}, f32[4,64,64]{2,1,0:T(8,128)S(1)}, ...), condition=%wide.region_3.4_spmd.clone, body=%wide.region_0.3_spmd.clone.sunk | while | flops 51646208 | bytes 2444416 | solution.py:98
  237.6 4.3 dynamic_update_slice.6
  244.2 4.3 dynamic_update_slice.6
  253.6 31.8 %all_gather.35 = f32[32,4,64]{2,1,0:T(4,128)} all-gather(f32[1,4,64]{2,1,0:T(4,128)S(1)} %all_gather.34), channel_id=1, replica_groups=mesh['seq'=32,'mp'=16] {'seq'}, dimensions={0}, use_global_device_ids=true | all-gather | bytes 33792 | tf_op jit(solution)/shard_map/all_gather | solution.py:24
  286.4 1.7 exponential_multiply_fusion
  294.1 26.7 %all-gather.18.cloned.1.call-done = f32[128,64,64]{2,1,0:T(8,128)} async-done(((f32[4,64,64]{2,1,0:T(8,128)}), f32[128,64,64]{2,1,0:T(8,128)}) %all-gather.18.cloned.1.call-update) | async-done | bytes 2097168 | tf_op jit(solution)/shard_map/all_gather | solution.py:24
  320.8 53.6 %while.30 = (s32[]{:T(128)}, f32[4,64]{1,0:T(4,128)S(1)}, f32[4,64,64]{2,1,0:T(8,128)S(1)}, s32[]{:T(128)}, f32[32,4,64]{2,1,0:T(4,128)}, /*index=5*/f32[32,4,64,64]{3,2,1,0:T(8,128)}, s32[]{:T(128)}, s32[]{:T(128)}) while((s32[]{:T(128)}, f32[4,64]{1,0:T(4,128)S(1)}, f32[4,64,64]{2,1,0:T(8,128)S(1)}, s32[]{:T(128)}, ...), condition=%wide.region_6.7_spmd.clone, body=%wide.region_5.6_spmd.clone.sunk | while | flops 66308 | bytes 201843 | solution.py:33
  374.5 1.9 fusion.42
  379.1 1.8 copy.183
  381.6 1.8 copy.182
  383.5 1.7 copy.180
  385.1 6.2 %all-gather.14.cloned.1.call-done = bf16[4096,256]{1,0:T(8,128)(2,1)} async-done(((bf16[128,256]{1,0:T(8,128)(2,1)}), bf16[4096,256]{1,0:T(8,128)(2,1)}) %all-gather.14.cloned.1.call-update) | async-done | bytes 2097168 | tf_op jit(solution)/shard_map/all_gather | solution.py:160
  391.3 72.5 %all-gather.16.cloned.1.call-done = bf16[256,4096]{1,0:T(8,128)(2,1)} async-done(((bf16[256,128]{1,0:T(8,128)(2,1)}), bf16[256,4096]{1,0:T(8,128)(2,1)}) %all-gather.16.cloned.1.call-update) | async-done | bytes 2097168 | tf_op jit(solution)/shard_map/all_gather | solution.py:239
  463.8 9.2 %fusion.63 = f32[256,4096]{1,0:T(8,128)} fusion(bf16[256,4096]{1,0:T(8,128)(2,1)} %all-gather.16.cloned.1.call-done, f32[256,256]{1,0:T(8,128)} %copy.183, f32[256,256]{1,0:T(8,128)} %copy.182, f32[128,256]{1,0:T(8,128)} %concatenate.31, f32[128,256]{1,0:T(8,128)} %copy.180, bf16[4096,256]{1,0:T(8,128)(2,1)} %all-gather.14.cloned.1.call-done, ...), kind=kOutput, calls=%fused_computation.83 | convolution fusion | flops 1086062592 | bytes 13388032 | tf_op jit(solution)/shard_map/dot_general | solution.py:241
  474.5 1.3 convolution_add_fusion.1
  476.6 85.1 %reduce-scatter.2.cloned.1.call-done = f32[16,4096]{1,0:T(8,128)} async-done(((f32[256,4096]{1,0:T(8,128)}), f32[16,4096]{1,0:T(8,128)}) %reduce-scatter.2.cloned.1.call-update) | async-done | bytes 262160 | tf_op jit(solution)/shard_map/reduce_scatter | solution.py:240
  561.7 1.6 convert_bitcast_fusion
  (228 shorter events, 88.0 us)
Async XLA Ops:
  7.2 73.5 %copy-start = (bf16[4096,128]{1,0:T(8,128)(2,1)S(1)}, bf16[4096,128]{1,0:T(8,128)(2,1)}, u32[]{:S(2)}) copy-start(bf16[4096,128]{1,0:T(8,128)(2,1)} %param.32) | copy-start | bytes 3145732
  7.2 80.2 %all-gather.12.cloned.1.call-start = ((), (), s32[]{:S(2)}) async-start(), calls=%async_computation.4 | async-start | bytes 2162688 | tf_op jit(solution)/shard_map/all_gather | solution.py:157
  7.9 149.5 %all-gather.8.cloned.1.call-start = ((), (), s32[]{:S(2)}) async-start(), calls=%async_computation.2 | async-start | bytes 2162688 | tf_op jit(solution)/shard_map/all_gather | solution.py:158
  13.4 12.5 %copy-start.16 = (f32[5,4096]{1,0:T(8,128)S(1)}, f32[5,4096]{1,0:T(8,128)}, u32[]{:S(2)}) copy-start(f32[5,4096]{1,0:T(8,128)} %param.26) | copy-start | bytes 245764
  13.4 13.3 %copy-start.19 = (bf16[256]{0:T(256)(128)(2,1)S(1)}, bf16[256]{0:T(256)(128)(2,1)}, u32[]{:S(2)}) copy-start(bf16[256]{0:T(256)(128)(2,1)} %param.24) | copy-start | bytes 1540
  13.4 53.6 %all-to-all-start = ((bf16[256,16,256]{2,0,1:T(8,128)(2,1)}), bf16[256,16,256]{2,0,1:T(8,128)(2,1)S(1)}, u32[]{:S(2)}, u32[]{:S(2)}) async-start(bf16[256,16,256]{2,0,1:T(8,128)(2,1)} %copy.154), calls=%async_computation | async-start | bytes 4194304 | tf_op jit(solution)/shard_map/all_to_all | solution.py:13
  22.9 205.3 %all-gather.10.cloned.1.call-start = ((), (), s32[]{:S(2)}) async-start(), calls=%async_computation.3 | async-start | bytes 2162688 | tf_op jit(solution)/shard_map/all_gather | solution.py:159
  23.7 297.1 %all-gather.18.cloned.1.call-start = ((), (), s32[]{:S(2)}) async-start(), calls=%async_computation.8 | async-start | bytes 4325376 | tf_op jit(solution)/shard_map/all_gather | solution.py:24
  24.6 2.2 collective-permute-start
  78.2 2.5 copy-start.3
  228.2 7.1 %copy-start.15 = (f32[4,64]{1,0:T(4,128)S(1)}, f32[4,64]{1,0:T(4,128)}, u32[]{:S(2)}) copy-start(f32[4,64]{1,0:T(4,128)} %param.34) | copy-start | bytes 3076
  235.4 15.5 %copy-start.20 = (s32[2]{0:T(128)S(1)}, s32[2]{0:T(128)}, u32[]{:S(2)}) copy-start(s32[2]{0:T(128)} %param.23) | copy-start | bytes 28
  235.4 16.2 %copy-start.11 = (f32[128,256]{0,1:T(8,128)S(1)}, f32[128,256]{0,1:T(8,128)}, u32[]{:S(2)}) copy-start(f32[128,256]{0,1:T(8,128)} %get-tuple-element.289) | copy-start | bytes 393220
  235.4 50.0 %copy-start.7 = (f32[128,256]{0,1:T(8,128)S(1)}, f32[128,256]{0,1:T(8,128)}, u32[]{:S(2)}) copy-start(f32[128,256]{0,1:T(8,128)} %get-tuple-element.290) | copy-start | bytes 393220
  248.9 0.7 copy-start.1
  248.9 36.6 %copy-start.10 = (f32[128,256]{0,1:T(8,128)S(1)}, f32[128,256]{0,1:T(8,128)}, u32[]{:S(2)}) copy-start(f32[128,256]{0,1:T(8,128)} %get-tuple-element.292) | copy-start | bytes 393220
  248.9 37.0 %copy-start.12 = (f32[128,256]{1,0:T(8,128)S(1)}, f32[128,256]{1,0:T(8,128)}, u32[]{:S(2)}) copy-start(f32[128,256]{1,0:T(8,128)} %get-tuple-element.296) | copy-start | bytes 393220
  249.6 141.7 %all-gather.14.cloned.1.call-start = ((), (), s32[]{:S(2)}) async-start(), calls=%async_computation.5 | async-start | bytes 2162688 | tf_op jit(solution)/shard_map/all_gather | solution.py:160
  250.2 213.6 %all-gather.16.cloned.1.call-start = ((), (), s32[]{:S(2)}) async-start(), calls=%async_computation.6 | async-start | bytes 2162688 | tf_op jit(solution)/shard_map/all_gather | solution.py:239
  250.8 310.9 %reduce-scatter.2.cloned.1.call-start = ((), (), s32[]{:S(2)}) async-start(), calls=%async_computation.7 | async-start | bytes 4456448 | tf_op jit(solution)/shard_map/reduce_scatter | solution.py:240
  250.9 34.4 %copy-start.17 = (f32[2,64]{1,0:T(2,128)}, f32[2,64]{1,0:T(2,128)S(1)}, u32[]{:S(2)}) copy-start(f32[2,64]{1,0:T(2,128)S(1)} %get-tuple-element.303) | copy-start | bytes 1540
  252.2 35.9 %copy-start.8 = (f32[2,64,4,64]{3,2,1,0:T(4,128)}, f32[2,64,4,64]{3,2,1,0:T(4,128)S(1)}, u32[]{:S(2)}) copy-start(f32[2,64,4,64]{3,2,1,0:T(4,128)S(1)} %fusion.67) | copy-start | bytes 393220
  288.1 2.4 copy-start.6
  288.1 2.6 copy-start.14
  374.5 89.4 %copy-start.4 = (bf16[256,16,256]{0,2,1:T(8,128)(2,1)S(1)}, bf16[256,16,256]{0,2,1:T(8,128)(2,1)}, u32[]{:S(2)}) copy-start(bf16[256,16,256]{0,2,1:T(8,128)(2,1)} %copy.155) | copy-start | bytes 6291460
  374.5 89.4 %copy-start.21 = (f32[256]{0:T(256)S(1)}, f32[256]{0:T(256)}, u32[]{:S(2)}) copy-start(f32[256]{0:T(256)} %param.36) | copy-start | bytes 3076
  374.5 89.3 %copy-start.22 = (f32[256]{0:T(256)S(1)}, f32[256]{0:T(256)}, u32[]{:S(2)}) copy-start(f32[256]{0:T(256)} %param.35) | copy-start | bytes 3076
  376.4 1.0 copy-start.5
  473.1 0.7 copy-start.18
  473.1 1.5 copy-start.9
  473.1 2.8 copy-start.2
  473.1 2.8 copy-start.13
Sparse Core Ops, SparseCore 0:
  10.1 76.1 all-gather.11
  88.5 68.8 all-gather.7
  159.5 68.6 all-gather.9
  249.7 71.0 all-gather.17
  322.8 68.4 all-gather.13
  393.2 70.5 all-gather.15
  473.2 88.4 reduce-scatter.1
